TPU v7x, 32 devices: a whole 2x2x4 slice. The times are simulated.
32 devices in a mesh: rep: 4 (over z), fsdp: 8 (over y, x, core).
Axes of the slice: x: 2, y: 2, z: 4, core: 2. Of those that a mesh axis runs over, the one named last changes fastest.
Arguments:
- tokens: bfloat16 [4096, 2048], P(('rep', 'fsdp')), may hold values from -6 to 6
- cotangent: bfloat16 [4096, 2048], P(('rep', 'fsdp')), may hold values from -6 to 6
- doc_lengths: int32 [4, 8], replicated, may hold values from 1 to 513, as said below
- norm1_gain: bfloat16 [2048], P('fsdp'), may hold values from 0.5 to 1.5
- w_query: bfloat16 [2048, 2048], P('fsdp'), may hold values from -0.125 to 0.125
- w_key: bfloat16 [2048, 256], P('fsdp'), may hold values from -0.125 to 0.125
- w_value: bfloat16 [2048, 256], P('fsdp'), may hold values from -0.125 to 0.125
- w_out: bfloat16 [2048, 2048], P('fsdp'), may hold values from -0.5 to 0.5
- norm2_gain: bfloat16 [2048], P('fsdp'), may hold values from 0.5 to 1.5
- w_gate: bfloat16 [2048, 5632], P('fsdp'), may hold values from -0.125 to 0.125
- w_up: bfloat16 [2048, 5632], P('fsdp'), may hold values from -0.125 to 0.125
- w_down: bfloat16 [5632, 2048], P('fsdp'), may hold values from -0.078125 to 0.078125
Outputs:
- output: bfloat16 [4096, 2048], P(('rep', 'fsdp'))
- grad_input: bfloat16 [4096, 2048], P(('rep', 'fsdp'))
- grad_norm1: float32 [2048], P('fsdp')
- grad_query: float32 [2048, 2048], P('fsdp')
- grad_key: float32 [2048, 256], P('fsdp')
- grad_value: float32 [2048, 256], P('fsdp')
- grad_out_proj: float32 [2048, 2048], P('fsdp')
- grad_norm2: float32 [2048], P('fsdp')
- grad_gate: float32 [2048, 5632], P('fsdp')
- grad_up: float32 [2048, 5632], P('fsdp')
- grad_down: float32 [5632, 2048], P('fsdp')
Inputs may be any that keep to these rules, and one draw needn't show every extreme that they name: `doc_lengths`: row s lists in order the lengths of the documents packed into sequence s, and as its last entry the length of the tail padding, at most 128; each row sums to 1024, and in each row exactly one document has 513 tokens.
All inputs are finite; a program needn't handle non-finite values.
Results may differ from a plain program's by a relative error of at most 0.022.
Values may be sent and summed in bfloat16 or wider, within the bound.
No kernel may reach another device: no remote copies, remote signals or barrier semaphores. Data moves between devices by JAX's collectives and lax.ppermute only.
A program may use at most 384 MiB of HBM per device.

v0:
```python
import math
import jax
import jax.numpy as jnp
from jax import lax
from jax.sharding import PartitionSpec as P

D = 2048
H = 32
KVH = 4
HD = 64
FF = 5632
DOCS = 8
NORM_EPS = 1e-05
ROPE_BASE = 10000.0
MASK_FILL = -1e30


def angle_tables(positions, head_dim):
    fractions = jnp.arange(0, head_dim, 2, dtype=jnp.float32) / head_dim
    inverse = jnp.exp(-math.log(ROPE_BASE) * fractions)
    angles = positions[:, None] * inverse[None, :]
    angles = jnp.concatenate([angles, angles], axis=-1)
    return (jnp.cos(angles)[:, None, :], jnp.sin(angles)[:, None, :])


def rotate(vectors, cos_table, sin_table):
    half_dim = vectors.shape[-1] // 2
    turned = jnp.concatenate([-vectors[..., half_dim:], vectors[..., :half_dim]], axis=-1)
    return vectors * cos_table + turned * sin_table


def rotate_back(gradients, cos_table, sin_table):
    half_dim = gradients.shape[-1] // 2
    moved = gradients * sin_table
    turned = jnp.concatenate([moved[..., half_dim:], -moved[..., :half_dim]], axis=-1)
    return gradients * cos_table + turned


def masks_for(lengths, offset, tok_count, seq_len):
    bounds = jnp.cumsum(lengths, dtype=jnp.int32)
    key_pos = jnp.arange(seq_len, dtype=jnp.int32)
    key_seg = jnp.sum(
        (bounds[None, :] <= key_pos[:, None]).astype(jnp.int32), axis=1, dtype=jnp.int32
    )
    key_valid = key_seg < DOCS - 1
    query_pos = offset + jnp.arange(tok_count, dtype=jnp.int32)
    query_seg = lax.dynamic_slice_in_dim(key_seg, offset, tok_count)
    query_valid = lax.dynamic_slice_in_dim(key_valid, offset, tok_count)
    allowed = (key_pos[None, :] <= query_pos[:, None]) & (query_seg[:, None] == key_seg[None, :])
    allowed = allowed & query_valid[:, None] & key_valid[None, :] | (
        key_pos[None, :] == query_pos[:, None]
    )
    return (allowed, query_valid, query_pos)


def masked_scores(query_grp, key_grp, allowed):
    score_scale = 1.0 / math.sqrt(query_grp.shape[-1])
    scores = (
        jnp.einsum("tgd,sd->tgs", query_grp, key_grp, preferred_element_type=jnp.float32)
        * score_scale
    )
    return jnp.where(allowed[:, None, :], scores, MASK_FILL)


def attend_forward(query_grp, key_grp, value_grp, allowed):
    scores = masked_scores(query_grp, key_grp, allowed)
    highest = jnp.max(scores, axis=-1, keepdims=True)
    weights = jnp.exp(scores - highest)
    totals = jnp.sum(weights, axis=-1, keepdims=True)
    prob_low = (weights / totals).astype(jnp.bfloat16)
    mixed = jnp.einsum("tgs,sd->tgd", prob_low, value_grp, preferred_element_type=jnp.float32)
    logsum = highest[..., 0] + jnp.log(totals[..., 0])
    return (mixed, logsum)


def attend_backward(query_grp, key_grp, value_grp, allowed, logsum, grad_mixed):
    score_scale = 1.0 / math.sqrt(query_grp.shape[-1])
    scores = masked_scores(query_grp, key_grp, allowed)
    probs_f32 = jnp.exp(scores - logsum[..., None])
    grad_probs = jnp.einsum(
        "tgd,sd->tgs", grad_mixed, value_grp, preferred_element_type=jnp.float32
    )
    inner_sum = jnp.sum(probs_f32 * grad_probs, axis=-1, keepdims=True)
    grad_scores = (probs_f32 * (grad_probs - inner_sum)).astype(jnp.bfloat16)
    grad_query = (
        jnp.einsum("tgs,sd->tgd", grad_scores, key_grp, preferred_element_type=jnp.float32)
        * score_scale
    )
    grad_key = (
        jnp.einsum("tgs,tgd->sd", grad_scores, query_grp, preferred_element_type=jnp.float32)
        * score_scale
    )
    grad_value = jnp.einsum(
        "tgs,tgd->sd",
        probs_f32.astype(jnp.bfloat16),
        grad_mixed,
        preferred_element_type=jnp.float32,
    )
    return (grad_query, grad_key, grad_value)


def norm_parts(vectors):
    scale_inv = lax.rsqrt(jnp.mean(vectors * vectors, axis=-1, keepdims=True) + NORM_EPS)
    return (scale_inv, vectors * scale_inv)


def norm_back(grad_hidden, normed, scale_inv, gain):
    grad_normed = grad_hidden * gain
    return scale_inv * (
        grad_normed - normed * jnp.mean(grad_normed * normed, axis=-1, keepdims=True)
    )


def local(
    tokens,
    cotangent,
    doc_lengths,
    norm1_gain,
    w_query,
    w_key,
    w_value,
    w_out,
    norm2_gain,
    w_gate,
    w_up,
    w_down,
):
    tok_rows = tokens.shape[0]
    group_size = lax.axis_size("fsdp")
    seq_len = tok_rows * group_size
    member = lax.axis_index("fsdp")
    replica = lax.axis_index("rep")
    offset = member * tok_rows
    lengths = lax.dynamic_index_in_dim(doc_lengths, replica, 0, keepdims=False)
    allowed, query_valid, query_pos = masks_for(lengths, offset, tok_rows, seq_len)
    valid_col = query_valid.astype(jnp.float32)[:, None]
    cos_table, sin_table = angle_tables(query_pos.astype(jnp.float32), HD)
    heads_per = H // KVH
    kv_width = KVH * HD
    gain_one, full_query, full_key, full_value, full_out = (
        lax.all_gather(norm1_gain, "fsdp", axis=0, tiled=True),
        lax.all_gather(w_query, "fsdp", axis=0, tiled=True),
        lax.all_gather(w_key, "fsdp", axis=0, tiled=True),
        lax.all_gather(w_value, "fsdp", axis=0, tiled=True),
        lax.all_gather(w_out, "fsdp", axis=0, tiled=True),
    )
    inputs = tokens.astype(jnp.float32)
    scale_one, normed_one = norm_parts(inputs)
    hidden_one = (normed_one * gain_one.astype(jnp.float32)).astype(jnp.bfloat16)
    queries = jnp.dot(hidden_one, full_query, preferred_element_type=jnp.float32).reshape(
        tok_rows, H, HD
    )
    key_proj = jnp.dot(hidden_one, full_key, preferred_element_type=jnp.float32).reshape(
        tok_rows, KVH, HD
    )
    value_low = jnp.dot(hidden_one, full_value, preferred_element_type=jnp.float32).astype(
        jnp.bfloat16
    )
    query_low = rotate(queries, cos_table, sin_table).astype(jnp.bfloat16)
    key_low = (
        rotate(key_proj, cos_table, sin_table).astype(jnp.bfloat16).reshape(tok_rows, kv_width)
    )
    kv_local = jnp.concatenate([key_low, value_low], axis=1)
    kv_seq = lax.all_gather(kv_local, "fsdp", axis=0, tiled=True)
    key_seq = kv_seq[:, :kv_width].reshape(seq_len, KVH, HD).transpose(1, 0, 2)
    value_seq = kv_seq[:, kv_width:].reshape(seq_len, KVH, HD).transpose(1, 0, 2)
    query_grp = query_low.reshape(tok_rows, KVH, heads_per, HD).transpose(1, 0, 2, 3)

    def forward_entry(packed):
        return attend_forward(packed[0], packed[1], packed[2], allowed)

    mixed, logsum = lax.map(forward_entry, (query_grp, key_seq, value_seq))
    attn_low = (mixed.transpose(1, 0, 2, 3).reshape(tok_rows, H * HD) * valid_col).astype(
        jnp.bfloat16
    )
    resid_one = inputs + jnp.dot(attn_low, full_out, preferred_element_type=jnp.float32)
    gain_two, full_gate, full_up, full_down = (
        lax.all_gather(norm2_gain, "fsdp", axis=0, tiled=True),
        lax.all_gather(w_gate, "fsdp", axis=0, tiled=True),
        lax.all_gather(w_up, "fsdp", axis=0, tiled=True),
        lax.all_gather(w_down, "fsdp", axis=0, tiled=True),
    )
    scale_two, normed_two = norm_parts(resid_one)
    hidden_two = (normed_two * gain_two.astype(jnp.float32)).astype(jnp.bfloat16)
    gate_pre = jnp.dot(hidden_two, full_gate, preferred_element_type=jnp.float32)
    up_pre = jnp.dot(hidden_two, full_up, preferred_element_type=jnp.float32)
    sigmoid_gate = jax.nn.sigmoid(gate_pre)
    silu_gate = gate_pre * sigmoid_gate
    inner_low = (silu_gate * up_pre).astype(jnp.bfloat16)
    result = (resid_one + jnp.dot(inner_low, full_down, preferred_element_type=jnp.float32)).astype(
        jnp.bfloat16
    )
    gain_one, full_query, full_key, full_value, full_out = (
        lax.all_gather(norm1_gain, "fsdp", axis=0, tiled=True),
        lax.all_gather(w_query, "fsdp", axis=0, tiled=True),
        lax.all_gather(w_key, "fsdp", axis=0, tiled=True),
        lax.all_gather(w_value, "fsdp", axis=0, tiled=True),
        lax.all_gather(w_out, "fsdp", axis=0, tiled=True),
    )
    gain_two, full_gate, full_up, full_down = (
        lax.all_gather(norm2_gain, "fsdp", axis=0, tiled=True),
        lax.all_gather(w_gate, "fsdp", axis=0, tiled=True),
        lax.all_gather(w_up, "fsdp", axis=0, tiled=True),
        lax.all_gather(w_down, "fsdp", axis=0, tiled=True),
    )
    grad_res = cotangent.astype(jnp.float32)
    grad_inner = jnp.einsum("td,fd->tf", cotangent, full_down, preferred_element_type=jnp.float32)
    grad_gate_low = (
        grad_inner * up_pre * sigmoid_gate * (1.0 + gate_pre * (1.0 - sigmoid_gate))
    ).astype(jnp.bfloat16)
    grad_up_low = (grad_inner * silu_gate).astype(jnp.bfloat16)
    grad_hidden_two = jnp.einsum(
        "tf,df->td", grad_gate_low, full_gate, preferred_element_type=jnp.float32
    )
    grad_hidden_two = grad_hidden_two + jnp.einsum(
        "tf,df->td", grad_up_low, full_up, preferred_element_type=jnp.float32
    )
    gain_two_local = jnp.sum(grad_hidden_two * normed_two, axis=0)
    grad_resid = grad_res + norm_back(
        grad_hidden_two, normed_two, scale_two, gain_two.astype(jnp.float32)
    )
    grad_attn_low = grad_resid.astype(jnp.bfloat16)
    grad_mix_low = jnp.einsum(
        "td,ed->te", grad_attn_low, full_out, preferred_element_type=jnp.float32
    ).astype(jnp.bfloat16)
    grad_mix_low = grad_mix_low * query_valid.astype(jnp.bfloat16)[:, None]
    grad_mix_grp = grad_mix_low.reshape(tok_rows, KVH, heads_per, HD).transpose(1, 0, 2, 3)

    def backward_entry(packed):
        return attend_backward(packed[0], packed[1], packed[2], allowed, packed[3], packed[4])

    grad_query_grp, grad_key_seq, grad_value_seq = lax.map(
        backward_entry, (query_grp, key_seq, value_seq, logsum, grad_mix_grp)
    )
    grad_queries = grad_query_grp.transpose(1, 0, 2, 3).reshape(tok_rows, H, HD)
    grad_query_low = (
        rotate_back(grad_queries, cos_table, sin_table)
        .reshape(tok_rows, H * HD)
        .astype(jnp.bfloat16)
    )
    kv_full = jnp.concatenate(
        [
            grad_key_seq.transpose(1, 0, 2).reshape(seq_len, kv_width),
            grad_value_seq.transpose(1, 0, 2).reshape(seq_len, kv_width),
        ],
        axis=1,
    )
    kv_grad = lax.psum_scatter(
        kv_full.astype(jnp.bfloat16), "fsdp", scatter_dimension=0, tiled=True
    ).astype(jnp.float32)
    grad_key_low = rotate_back(
        kv_grad[:, :kv_width].reshape(tok_rows, KVH, HD), cos_table, sin_table
    )
    grad_key_low = grad_key_low.reshape(tok_rows, kv_width).astype(jnp.bfloat16)
    grad_value_low = kv_grad[:, kv_width:].astype(jnp.bfloat16)
    grad_hidden_one = jnp.einsum(
        "te,de->td", grad_query_low, full_query, preferred_element_type=jnp.float32
    )
    grad_hidden_one = grad_hidden_one + jnp.einsum(
        "te,de->td", grad_key_low, full_key, preferred_element_type=jnp.float32
    )
    grad_hidden_one = grad_hidden_one + jnp.einsum(
        "te,de->td", grad_value_low, full_value, preferred_element_type=jnp.float32
    )
    gain_one_local = jnp.sum(grad_hidden_one * normed_one, axis=0)
    grad_inputs = (
        grad_resid + norm_back(grad_hidden_one, normed_one, scale_one, gain_one.astype(jnp.float32))
    ).astype(jnp.bfloat16)
    grad_qkv_cols = jnp.concatenate([grad_query_low, grad_key_low, grad_value_low], axis=1)
    grad_gate_up_cols = jnp.concatenate([grad_gate_low, grad_up_low], axis=1)
    gain_one_part, gain_two_part = (
        lax.psum_scatter(gain_one_local, "fsdp", scatter_dimension=0, tiled=True),
        lax.psum_scatter(gain_two_local, "fsdp", scatter_dimension=0, tiled=True),
    )
    part_qkv = lax.psum_scatter(
        jnp.einsum(
            "tc,tk->ck", hidden_one, grad_qkv_cols, preferred_element_type=jnp.float32
        ).astype(jnp.bfloat16),
        "fsdp",
        scatter_dimension=0,
        tiled=True,
    )
    part_out = lax.psum_scatter(
        jnp.einsum("tc,tk->ck", attn_low, grad_attn_low, preferred_element_type=jnp.float32).astype(
            jnp.bfloat16
        ),
        "fsdp",
        scatter_dimension=0,
        tiled=True,
    )
    part_gate_up = lax.psum_scatter(
        jnp.einsum(
            "tc,tk->ck", hidden_two, grad_gate_up_cols, preferred_element_type=jnp.float32
        ).astype(jnp.bfloat16),
        "fsdp",
        scatter_dimension=0,
        tiled=True,
    )
    part_down = lax.psum_scatter(
        jnp.einsum("tc,tk->ck", inner_low, cotangent, preferred_element_type=jnp.float32).astype(
            jnp.bfloat16
        ),
        "fsdp",
        scatter_dimension=0,
        tiled=True,
    )
    summed = (
        lax.psum(gain_one_part.astype(jnp.bfloat16), "rep").astype(jnp.float32),
        lax.psum(part_qkv, "rep").astype(jnp.float32),
        lax.psum(part_out, "rep").astype(jnp.float32),
        lax.psum(gain_two_part.astype(jnp.bfloat16), "rep").astype(jnp.float32),
        lax.psum(part_gate_up, "rep").astype(jnp.float32),
        lax.psum(part_down, "rep").astype(jnp.float32),
    )
    grad_norm_one, grad_qkv, grad_out_part, grad_norm_two, grad_gate_up, grad_down_part = summed
    grad_query_part = grad_qkv[:, :D]
    grad_key_part = grad_qkv[:, D : D + kv_width]
    grad_value_part = grad_qkv[:, D + kv_width :]
    grad_gate_part = grad_gate_up[:, :FF]
    grad_up_part = grad_gate_up[:, FF:]
    return (
        result,
        grad_inputs,
        grad_norm_one,
        grad_query_part,
        grad_key_part,
        grad_value_part,
        grad_out_part,
        grad_norm_two,
        grad_gate_part,
        grad_up_part,
        grad_down_part,
    )


def solution(mesh):
    placed = (
        P(("rep", "fsdp"), None),
        P(("rep", "fsdp"), None),
        P(),
        P("fsdp"),
        P("fsdp", None),
        P("fsdp", None),
        P("fsdp", None),
        P("fsdp", None),
        P("fsdp"),
        P("fsdp", None),
        P("fsdp", None),
        P("fsdp", None),
    )
    return jax.shard_map(
        local,
        mesh=mesh,
        in_specs=placed,
        out_specs=(
            P(("rep", "fsdp"), None),
            P(("rep", "fsdp"), None),
            P("fsdp"),
            P("fsdp", None),
            P("fsdp", None),
            P("fsdp", None),
            P("fsdp", None),
            P("fsdp"),
            P("fsdp", None),
            P("fsdp", None),
            P("fsdp", None),
        ),
        check_vma=False,
    )
```

profile of v0, /device:TPU:0, one launch (start us, length us, event | category | flops | bytes accessed | tf_op | source)
XLA Modules:
  0.0 1672.1 jit_solution(14276761914154948728)
XLA Ops:
  9.4 10.3 all-gather
  21.3 14.8 all-gather.13.cloned.1.call-done
  38.2 23.4 %all-gather.15.cloned.1.call-done = bf16[2048,256]{1,0:T(8,128)(2,1)} async-done(((bf16[256,256]{1,0:T(8,128)(2,1)}), bf16[2048,256]{1,0:T(8,128)(2,1)}) %all-gather.15.cloned.1.call-update) | async-done | bytes 1048592 | tf_op jit(solution)/shard_map/all_gather | solution.py:144
  67.7 8.8 all-gather.1
  76.5 11.1 all-gather.17.cloned.1.call-done
  89.3 54.5 %all-gather.11.cloned.1.call-done = bf16[2048,2048]{1,0:T(8,128)(2,1)} async-done(((bf16[256,2048]{1,0:T(8,128)(2,1)}), bf16[2048,2048]{1,0:T(8,128)(2,1)}) %all-gather.11.cloned.1.call-update) | async-done | bytes 8388624 | tf_op jit(solution)/shard_map/all_gather | solution.py:142
  143.7 6.9 fusion.108
  151.1 14.7 while.28
  168.4 31.5 %all-gather.19.cloned.1.call-done = bf16[2048,2048]{1,0:T(8,128)(2,1)} async-done(((bf16[256,2048]{1,0:T(8,128)(2,1)}), bf16[2048,2048]{1,0:T(8,128)(2,1)}) %all-gather.19.cloned.1.call-update) | async-done | bytes 8388624 | tf_op jit(solution)/shard_map/all_gather | solution.py:145
  204.8 113.3 %all-gather.21.cloned.1.call-done = bf16[2048,5632]{1,0:T(8,128)(2,1)} async-done(((bf16[256,5632]{1,0:T(8,128)(2,1)}), bf16[2048,5632]{1,0:T(8,128)(2,1)}) %all-gather.21.cloned.1.call-update) | async-done | bytes 23068688 | tf_op jit(solution)/shard_map/all_gather | solution.py:179
  318.1 12.3 fusion.117
  330.4 106.1 %all-gather.23.cloned.1.call-done = bf16[2048,5632]{1,0:T(8,128)(2,1)} async-done(((bf16[256,5632]{1,0:T(8,128)(2,1)}), bf16[2048,5632]{1,0:T(8,128)(2,1)}) %all-gather.23.cloned.1.call-update) | async-done | bytes 23068688 | tf_op jit(solution)/shard_map/all_gather | solution.py:180
  436.5 12.3 fusion.118
  448.8 106.1 %all-gather.25.cloned.1.call-done = bf16[5632,2048]{1,0:T(8,128)(2,1)} async-done(((bf16[704,2048]{1,0:T(8,128)(2,1)}), bf16[5632,2048]{1,0:T(8,128)(2,1)}) %all-gather.25.cloned.1.call-update) | async-done | bytes 23068688 | tf_op jit(solution)/shard_map/all_gather | solution.py:181
  554.9 15.0 multiply_convert_fusion.1
  569.8 12.3 fusion.119
  582.1 13.2 multiply_reduce_fusion.1
  597.1 7.1 fusion.71
  607.3 42.8 %while.29 = (s32[]{:T(128)}, f32[4,128,8,64]{1,3,2,0:T(8,128)}, bf16[4,1024,64]{1,2,0:T(8,128)(2,1)}, bf16[4,1024,64]{1,2,0:T(8,128)(2,1)}, bf16[4,128,8,64]{1,3...) while((s32[]{:T(128)}, f32[4,128,8,64]{1,3,2,0:T(8,128)}, ...), condition=%wide.region_11.12_spmd.clone, body=%wide.region_9.11_spmd.clone.sunk | while | flops 687864832 | bytes 44211620 | solution.py:232
  663.0 27.9 %reduce-scatter.16.cloned.1.call-done = bf16[128,512]{1,0:T(8,128)(2,1)} async-done(((bf16[1024,512]{1,0:T(8,128)(2,1)}), bf16[128,512]{1,0:T(8,128)(2,1)}) %reduce-scatter.16.cloned.1.call-update) | async-done | bytes 131088
  692.1 6.6 convolution_convert_fusion.2
  699.9 14.0 convolution_convert_fusion.1
  715.0 20.3 %convolution_convert_fusion = bf16[2048,11264]{1,0:T(8,128)(2,1)} fusion(bf16[128,2048]{1,0:T(8,128)(2,1)S(1)} %copy-done.9, bf16[128,5632]{1,0:T(8,128)(2,1)} %get-tuple-element.242, bf16[128,5632]{1,0:T(8,128)(2,1)} %get-tuple-element.243), kind=kOutput, calls=%fused_computation.73 | convolution fusion | flops 5934415872 | bytes 49545216 | tf_op jit(solution)/shard_map/tc,tk->ck/dot_general | solution.py:292
  735.6 29.9 %reduce-scatter.12.cloned.1.call-done = bf16[256,2048]{1,0:T(8,128)(2,1)} async-done(((bf16[2048,2048]{1,0:T(8,128)(2,1)}), bf16[256,2048]{1,0:T(8,128)(2,1)}) %reduce-scatter.12.cloned.1.call-update) | async-done | bytes 1048592 | tf_op jit(solution)/shard_map/reduce_scatter | solution.py:283
  765.5 85.5 %reduce-scatter.10.cloned.1.call-done = bf16[256,2560]{1,0:T(8,128)(2,1)} async-done(((bf16[2048,2560]{1,0:T(8,128)(2,1)}), bf16[256,2560]{1,0:T(8,128)(2,1)}) %reduce-scatter.10.cloned.1.call-update) | async-done | bytes 1310736 | tf_op jit(solution)/shard_map/reduce_scatter | solution.py:275
  851.0 149.8 %reduce-scatter.14.cloned.1.call-done = bf16[704,2048]{1,0:T(8,128)(2,1)} async-done(((bf16[5632,2048]{1,0:T(8,128)(2,1)}), bf16[704,2048]{1,0:T(8,128)(2,1)}) %reduce-scatter.14.cloned.1.call-update) | async-done | bytes 2883600 | tf_op jit(solution)/shard_map/reduce_scatter | solution.py:299
  1000.9 268.4 %reduce-scatter.18.cloned.1.call-done = bf16[256,11264]{1,0:T(8,128)(2,1)} async-done(((bf16[2048,11264]{1,0:T(8,128)(2,1)}), bf16[256,11264]{1,0:T(8,128)(2,1)}) %reduce-scatter.18.cloned.1.call-update) | async-done | bytes 5767184
  1271.2 6.4 fusion.120
  1277.7 12.0 fusion.70
  1290.8 25.4 %all-reduce.3 = (bf16[2048]{0:T(1024)(128)(2,1)S(1)}, bf16[2048]{0:T(1024)(128)(2,1)S(1)}) all-reduce(f32[2048]{0:T(1024)S(1)} %get-tuple-element.174, f32[2048]{0:T(1024)S(1)} %get-tuple-element.172), channel_id=3, replica_groups=mesh['rep'=4,'fsdp'=8] {'fsdp'}, use_global_device_ids=true, to_apply=%region_15.16.clone | all-reduce | flops 4096 | bytes 24576
  1316.4 12.4 all-reduce.4
  1331.1 318.6 %all-reduce.8.cloned.1.call-done = (bf16[256,2560]{1,0:T(8,128)(2,1)}, bf16[256,2048]{1,0:T(8,128)(2,1)}, bf16[256,11264]{1,0:T(8,128)(2,1)}, bf16[704,2048]{1,0:T(8,128)(2,1)}) async-done(((bf16[256,2560]{1,0:T(8,128)(2,1)}, bf16[256,2048]{1,0:T(8,128)(2,1)}, bf16[256,11264]{1,0:T(8,128)(2,1)}, bf16[704,2048]{1,0:T(8,128)(2,1)}), (bf16[256,2560]{1,0:T(8,128)(2,1)}, bf16[256,2048]{1,0:T(8,128)(2,1)}, ...) | async-done | bytes 11010064 | tf_op jit(solution)/shard_map/psum | solution.py:309
  (258 shorter events, 119.4 us)
Async XLA Ops:
  7.2 60.0 %copy-start = (s32[4,8]{1,0:T(4,128)S(1)}, s32[4,8]{1,0:T(4,128)}, u32[]{:S(2)}) copy-start(s32[4,8]{1,0:T(4,128)} %param.18) | copy-start | bytes 388
  7.2 54.4 %copy-start.3 = (bf16[128,2048]{1,0:T(8,128)(2,1)S(1)}, bf16[128,2048]{1,0:T(8,128)(2,1)}, u32[]{:S(2)}) copy-start(bf16[128,2048]{1,0:T(8,128)(2,1)} %param.16) | copy-start | bytes 1572868
  7.2 28.9 %all-gather.13.cloned.1.call-start = ((), (), s32[]{:S(2)}) async-start(), calls=%async_computation.6 | async-start | bytes 1179648 | tf_op jit(solution)/shard_map/all_gather | solution.py:143
  7.9 53.6 %all-gather.15.cloned.1.call-start = ((), (), s32[]{:S(2)}) async-start(), calls=%async_computation.7 | async-start | bytes 1179648 | tf_op jit(solution)/shard_map/all_gather | solution.py:144
  8.7 78.9 %all-gather.17.cloned.1.call-start = ((), (), s32[]{:S(2)}) async-start(), calls=%async_computation.8 | async-start | bytes 1179648 | tf_op jit(solution)/shard_map/all_gather | solution.py:164
  19.8 124.0 %copy-start.31 = (f32[8,1,256]{2,1,0:T(1,128)}, f32[8,1,256]{2,1,0:T(1,128)S(1)}, u32[]{:S(2)}) copy-start(f32[8,1,256]{2,1,0:T(1,128)S(1)} %convert_element_type.160) | copy-start | bytes 24580
  19.9 130.7 %copy-start.23 = (f32[128,64]{0,1:T(8,128)}, f32[128,64]{0,1:T(8,128)S(1)}, u32[]{:S(2)}) copy-start(f32[128,64]{0,1:T(8,128)S(1)} %get-tuple-element.260) | copy-start | bytes 98308
  20.0 130.7 %copy-start.25 = (f32[128,64]{0,1:T(8,128)}, f32[128,64]{0,1:T(8,128)S(1)}, u32[]{:S(2)}) copy-start(f32[128,64]{0,1:T(8,128)S(1)} %get-tuple-element.259) | copy-start | bytes 98308
  21.3 122.4 %copy-start.34 = (f32[128]{0:T(128)}, f32[128]{0:T(128)S(1)}, u32[]{:S(2)}) copy-start(f32[128]{0:T(128)S(1)} %add_rsqrt_fusion.1) | copy-start | bytes 1540
  63.8 79.9 %all-gather.11.cloned.1.call-start = ((), (), s32[]{:S(2)}) async-start(), calls=%async_computation.5 | async-start | bytes 9437184 | tf_op jit(solution)/shard_map/all_gather | solution.py:142
  64.4 135.5 %all-gather.19.cloned.1.call-start = ((), (), s32[]{:S(2)}) async-start(), calls=%async_computation.9 | async-start | bytes 9437184 | tf_op jit(solution)/shard_map/all_gather | solution.py:145
  65.0 253.1 %all-gather.21.cloned.1.call-start = ((), (), s32[]{:S(2)}) async-start(), calls=%async_computation.10 | async-start | bytes 25952256 | tf_op jit(solution)/shard_map/all_gather | solution.py:179
  65.6 370.9 %all-gather.23.cloned.1.call-start = ((), (), s32[]{:S(2)}) async-start(), calls=%async_computation.11 | async-start | bytes 25952256 | tf_op jit(solution)/shard_map/all_gather | solution.py:180
  66.4 488.5 %all-gather.25.cloned.1.call-start = ((), (), s32[]{:S(2)}) async-start(), calls=%async_computation.12 | async-start | bytes 25952256 | tf_op jit(solution)/shard_map/all_gather | solution.py:181
  67.1 623.8 %reduce-scatter.16.cloned.1.call-start = ((), (), s32[]{:S(2)}) async-start(), calls=%async_computation.16 | async-start | bytes 1179648
  168.4 36.2 %copy-start.6 = (bf16[128,2048]{0,1:T(8,128)(2,1)}, bf16[128,2048]{0,1:T(8,128)(2,1)S(1)}, u32[]{:S(2)}) copy-start(bf16[128,2048]{0,1:T(8,128)(2,1)S(1)} %fusion.88) | copy-start | bytes 1572868
  204.8 231.7 %copy-start.8 = (bf16[128,2048]{1,0:T(8,128)(2,1)}, bf16[128,2048]{1,0:T(8,128)(2,1)S(1)}, u32[]{:S(2)}) copy-start(bf16[128,2048]{1,0:T(8,128)(2,1)S(1)} %multiply_convert_fusion.4) | copy-start | bytes 1572868
  330.4 224.4 %copy-start.18 = (bf16[128,2048]{1,0:T(8,128)(2,1)S(1)}, bf16[128,2048]{1,0:T(8,128)(2,1)}, u32[]{:S(2)}) copy-start(bf16[128,2048]{1,0:T(8,128)(2,1)} %param.17) | copy-start | bytes 1572868
  569.8 12.3 copy-start.5
  654.7 110.8 %reduce-scatter.12.cloned.1.call-start = ((), (), s32[]{:S(2)}) async-start(), calls=%async_computation.14 | async-start | bytes 9437184 | tf_op jit(solution)/shard_map/reduce_scatter | solution.py:283
  660.5 190.6 %reduce-scatter.10.cloned.1.call-start = ((), (), s32[]{:S(2)}) async-start(), calls=%async_computation.13 | async-start | bytes 11796480 | tf_op jit(solution)/shard_map/reduce_scatter | solution.py:275
  662.6 29.5 %copy-start.32 = (f32[8,1,256]{2,1,0:T(1,128)S(1)}, f32[8,1,256]{2,1,0:T(1,128)}, u32[]{:S(2)}) copy-start(f32[8,1,256]{2,1,0:T(1,128)} %copy-done.31) | copy-start | bytes 24580
  662.6 29.5 %copy-start.35 = (f32[128]{0:T(128)S(1)}, f32[128]{0:T(128)}, u32[]{:S(2)}) copy-start(f32[128]{0:T(128)} %copy-done.34) | copy-start | bytes 1540
  663.0 35.8 %copy-start.12 = (bf16[128,2048]{0,1:T(8,128)(2,1)}, bf16[128,2048]{0,1:T(8,128)(2,1)S(1)}, u32[]{:S(2)}) copy-start(bf16[128,2048]{0,1:T(8,128)(2,1)S(1)} %fusion.87) | copy-start | bytes 1572868
  698.8 302.1 %reduce-scatter.14.cloned.1.call-start = ((), (), s32[]{:S(2)}) async-start(), calls=%async_computation.15 | async-start | bytes 25952256 | tf_op jit(solution)/shard_map/reduce_scatter | solution.py:299
  714.0 555.3 %reduce-scatter.18.cloned.1.call-start = ((), (), s32[]{:S(2)}) async-start(), calls=%async_computation.17 | async-start | bytes 51904512
  735.4 914.3 %all-reduce.8.cloned.1.call-start = ((), (), s32[]{:S(2)}) async-start(), calls=%async_computation.18 | async-start | bytes 22020096 | tf_op jit(solution)/shard_map/psum | solution.py:309
  1271.2 6.5 copy-start.11
  1277.6 12.1 copy-start.20
  1277.6 12.5 copy-start.22
  1277.7 12.5 copy-start.33
  1649.7 6.4 copy-start.2
  (35 other events, 74.7 us)
Sparse Core Ops, SparseCore 0:
  9.9 26.1 all-gather.12
  38.0 23.4 all-gather.14
  64.0 23.4 all-gather.16
  89.3 54.3 all-gather.10
  145.5 54.3 all-gather.18
  201.6 116.4 all-gather.20
  320.0 116.4 all-gather.22
  438.4 116.4 all-gather.24
  654.8 36.0 reduce-scatter.15
  694.2 71.2 reduce-scatter.11
  769.4 81.5 reduce-scatter.9
  854.9 145.8 reduce-scatter.13
  1004.9 264.2 reduce-scatter.17
  1272.0 377.6 all-reduce.7
where the time goes:
time: 1680 us; the launch traced here: 1670 us
  waiting for transfers between devices  1350 us (80%)
  matrix products  195 us (12%)
  blocking collectives  57 us (3%)
  other arithmetic  29.4 us (2%)
  local copies, waits for them, and re-layouts  28.5 us (2%)
    psum x1, waiting for transfers between devices, local(): lax.psum(part_qkv, 'rep').astype(jnp.float32)  319 us
    unnamed x16, waiting for transfers between devices  301 us
    reduce_scatter x1, waiting for transfers between devices, local(): lax.psum_scatter(jnp.einsum('tc,tk->ck', inner_low, cotangent, preferred_...  150 us
    all_gather x1, waiting for transfers between devices, local(): lax.all_gather(w_gate, 'fsdp', axis=0, tiled=True)  113 us
    all_gather x1, waiting for transfers between devices, local(): lax.all_gather(w_up, 'fsdp', axis=0, tiled=True)  106 us
    all_gather x1, waiting for transfers between devices, local(): lax.all_gather(w_down, 'fsdp', axis=0, tiled=True)  106 us
    reduce_scatter x1, waiting for transfers between devices, local(): lax.psum_scatter(jnp.einsum('tc,tk->ck', hidden_one, grad_qkv_cols, prefe...  85.5 us
    all_gather x1, waiting for transfers between devices, local(): lax.all_gather(w_query, 'fsdp', axis=0, tiled=True)  54.5 us
  transfers between devices with their start and end apart: 14, of which 14 were waited for; matrix products, arithmetic and copies ran while one was open for 8% of the time, Pallas kernels for 0%

commit v1 on v0

--- a/solution.py
+++ b/solution.py
@@ -304,9 +304,10 @@
         scatter_dimension=0,
         tiled=True,
     )
+    remake_figure_all = lambda v0, named_axis: jnp.sum(lax.all_gather(v0, named_axis), axis=0)
     summed = (
         lax.psum(gain_one_part.astype(jnp.bfloat16), "rep").astype(jnp.float32),
-        lax.psum(part_qkv, "rep").astype(jnp.float32),
+        remake_figure_all(part_qkv, "rep").astype(jnp.float32),
         lax.psum(part_out, "rep").astype(jnp.float32),
         lax.psum(gain_two_part.astype(jnp.bfloat16), "rep").astype(jnp.float32),
         lax.psum(part_gate_up, "rep").astype(jnp.float32),

time: 1680 us -> 1740 us (1.036)
  waiting for transfers between devices: 1350 us -> 1400 us
    reduce_scatter x1, waiting for transfers between devices: 85.5 us -> 38 us  [local(): lax.psum_scatter(jnp.einsum('tc,tk->ck', hidden_one, grad_qkv_cols, prefe...]
    reduce_scatter x1, waiting for transfers between devices: 29.9 us -> 74.5 us  [local(): lax.psum_scatter(jnp.einsum('tc,tk->ck', attn_low, grad_attn_low, preferr...]
    all_gather x0 -> x1, waiting for transfers between devices: none -> 38 us  [local(): lax.all_gather(v0, named_axis)]
    unnamed x16 -> x17, waiting for transfers between devices: 301 us -> 307 us
  transfers between devices with their start and end apart: 14 -> 15, of which waited for: 14 -> 15; matrix products, arithmetic and copies ran while one was open for 8% -> 8% of each run, Pallas kernels for 0% -> 0%
where the time goes in v1:
time: 1740 us; the launch traced here: 1730 us
  waiting for transfers between devices  1400 us (80%)
  matrix products  196 us (11%)
  blocking collectives  56.3 us (3%)
  other arithmetic  34.6 us (2%)
  local copies, waits for them, and re-layouts  29.2 us (2%)
    psum x1, waiting for transfers between devices, local(): lax.psum(part_out, 'rep').astype(jnp.float32)  329 us
    unnamed x17, waiting for transfers between devices  307 us
    reduce_scatter x1, waiting for transfers between devices, local(): lax.psum_scatter(jnp.einsum('tc,tk->ck', inner_low, cotangent, preferred_...  150 us
    all_gather x1, waiting for transfers between devices, local(): lax.all_gather(w_gate, 'fsdp', axis=0, tiled=True)  113 us
    all_gather x1, waiting for transfers between devices, local(): lax.all_gather(w_down, 'fsdp', axis=0, tiled=True)  106 us
    all_gather x1, waiting for transfers between devices, local(): lax.all_gather(w_up, 'fsdp', axis=0, tiled=True)  106 us
    reduce_scatter x1, waiting for transfers between devices, local(): lax.psum_scatter(jnp.einsum('tc,tk->ck', attn_low, grad_attn_low, preferr...  74.5 us
    all_gather x1, waiting for transfers between devices, local(): lax.all_gather(w_query, 'fsdp', axis=0, tiled=True)  54.5 us
  transfers between devices with their start and end apart: 15, of which 15 were waited for; matrix products, arithmetic and copies ran while one was open for 8% of the time, Pallas kernels for 0%

profile of v1, /device:TPU:0, one launch (start us, length us, event | category | flops | bytes accessed | tf_op | source)
XLA Modules:
  0.0 1730.5 jit_solution(1383590045544846180)
XLA Ops:
  9.4 10.3 all-gather.1
  21.3 14.8 all-gather.15.cloned.1.call-done
  38.2 23.4 %all-gather.17.cloned.1.call-done = bf16[2048,256]{1,0:T(8,128)(2,1)} async-done(((bf16[256,256]{1,0:T(8,128)(2,1)}), bf16[2048,256]{1,0:T(8,128)(2,1)}) %all-gather.17.cloned.1.call-update) | async-done | bytes 1048592 | tf_op jit(solution)/shard_map/all_gather | solution.py:144
  67.7 8.8 all-gather.2
  76.5 11.1 all-gather.19.cloned.1.call-done
  89.3 54.5 %all-gather.13.cloned.1.call-done = bf16[2048,2048]{1,0:T(8,128)(2,1)} async-done(((bf16[256,2048]{1,0:T(8,128)(2,1)}), bf16[2048,2048]{1,0:T(8,128)(2,1)}) %all-gather.13.cloned.1.call-update) | async-done | bytes 8388624 | tf_op jit(solution)/shard_map/all_gather | solution.py:142
  143.7 6.9 fusion.108
  151.1 14.7 while.28
  168.4 31.4 %all-gather.21.cloned.1.call-done = bf16[2048,2048]{1,0:T(8,128)(2,1)} async-done(((bf16[256,2048]{1,0:T(8,128)(2,1)}), bf16[2048,2048]{1,0:T(8,128)(2,1)}) %all-gather.21.cloned.1.call-update) | async-done | bytes 8388624 | tf_op jit(solution)/shard_map/all_gather | solution.py:145
  204.8 113.3 %all-gather.23.cloned.1.call-done = bf16[2048,5632]{1,0:T(8,128)(2,1)} async-done(((bf16[256,5632]{1,0:T(8,128)(2,1)}), bf16[2048,5632]{1,0:T(8,128)(2,1)}) %all-gather.23.cloned.1.call-update) | async-done | bytes 23068688 | tf_op jit(solution)/shard_map/all_gather | solution.py:179
  318.1 12.3 fusion.117
  330.4 106.1 %all-gather.25.cloned.1.call-done = bf16[2048,5632]{1,0:T(8,128)(2,1)} async-done(((bf16[256,5632]{1,0:T(8,128)(2,1)}), bf16[2048,5632]{1,0:T(8,128)(2,1)}) %all-gather.25.cloned.1.call-update) | async-done | bytes 23068688 | tf_op jit(solution)/shard_map/all_gather | solution.py:180
  436.5 12.3 fusion.118
  448.8 106.1 %all-gather.27.cloned.1.call-done = bf16[5632,2048]{1,0:T(8,128)(2,1)} async-done(((bf16[704,2048]{1,0:T(8,128)(2,1)}), bf16[5632,2048]{1,0:T(8,128)(2,1)}) %all-gather.27.cloned.1.call-update) | async-done | bytes 23068688 | tf_op jit(solution)/shard_map/all_gather | solution.py:181
  554.9 15.0 multiply_convert_fusion.1
  569.8 12.2 fusion.119
  582.1 13.2 multiply_reduce_fusion.1
  597.1 7.1 fusion.71
  607.3 42.8 %while.29 = (s32[]{:T(128)}, f32[4,128,8,64]{1,3,2,0:T(8,128)}, bf16[4,1024,64]{1,2,0:T(8,128)(2,1)}, bf16[4,1024,64]{1,2,0:T(8,128)(2,1)}, bf16[4,128,8,64]{1,3...) while((s32[]{:T(128)}, f32[4,128,8,64]{1,3,2,0:T(8,128)}, ...), condition=%wide.region_11.12_spmd.clone, body=%wide.region_9.11_spmd.clone.sunk | while | flops 687864832 | bytes 44211620 | solution.py:232
  656.6 34.3 %reduce-scatter.16.cloned.1.call-done = bf16[128,512]{1,0:T(8,128)(2,1)} async-done(((bf16[1024,512]{1,0:T(8,128)(2,1)}), bf16[128,512]{1,0:T(8,128)(2,1)}) %reduce-scatter.16.cloned.1.call-update) | async-done | bytes 131088
  707.0 14.1 convolution_convert_fusion.1
  722.1 20.4 %convolution_convert_fusion = bf16[2048,11264]{1,0:T(8,128)(2,1)} fusion(bf16[128,2048]{1,0:T(8,128)(2,1)S(1)} %copy-done.8, bf16[128,5632]{1,0:T(8,128)(2,1)} %get-tuple-element.241, bf16[128,5632]{1,0:T(8,128)(2,1)} %get-tuple-element.242), kind=kOutput, calls=%fused_computation.73 | convolution fusion | flops 5934415872 | bytes 49545216 | tf_op jit(solution)/shard_map/tc,tk->ck/dot_general | solution.py:292
  742.6 38.0 %reduce-scatter.10.cloned.1.call-done = bf16[256,2560]{1,0:T(8,128)(2,1)} async-done(((bf16[2048,2560]{1,0:T(8,128)(2,1)}), bf16[256,2560]{1,0:T(8,128)(2,1)}) %reduce-scatter.10.cloned.1.call-update) | async-done | bytes 1310736 | tf_op jit(solution)/shard_map/reduce_scatter | solution.py:275
  780.9 74.5 %reduce-scatter.12.cloned.1.call-done = bf16[256,2048]{1,0:T(8,128)(2,1)} async-done(((bf16[2048,2048]{1,0:T(8,128)(2,1)}), bf16[256,2048]{1,0:T(8,128)(2,1)}) %reduce-scatter.12.cloned.1.call-update) | async-done | bytes 1048592 | tf_op jit(solution)/shard_map/reduce_scatter | solution.py:283
  855.3 149.8 %reduce-scatter.14.cloned.1.call-done = bf16[704,2048]{1,0:T(8,128)(2,1)} async-done(((bf16[5632,2048]{1,0:T(8,128)(2,1)}), bf16[704,2048]{1,0:T(8,128)(2,1)}) %reduce-scatter.14.cloned.1.call-update) | async-done | bytes 2883600 | tf_op jit(solution)/shard_map/reduce_scatter | solution.py:299
  1005.2 268.4 %reduce-scatter.18.cloned.1.call-done = bf16[256,11264]{1,0:T(8,128)(2,1)} async-done(((bf16[2048,11264]{1,0:T(8,128)(2,1)}), bf16[256,11264]{1,0:T(8,128)(2,1)}) %reduce-scatter.18.cloned.1.call-update) | async-done | bytes 5767184
  1282.0 12.6 fusion.70
  1295.7 25.1 %all-reduce.3 = (bf16[2048]{0:T(1024)(128)(2,1)S(1)}, bf16[2048]{0:T(1024)(128)(2,1)S(1)}) all-reduce(f32[2048]{0:T(1024)S(1)} %get-tuple-element.174, f32[2048]{0:T(1024)S(1)} %get-tuple-element.172), channel_id=4, replica_groups=mesh['rep'=4,'fsdp'=8] {'fsdp'}, use_global_device_ids=true, to_apply=%region_15.16.clone | all-reduce | flops 4096 | bytes 24576
  1321.0 12.1 all-reduce.4
  1335.3 38.0 %all-gather.29.cloned.1.call-done = bf16[1024,2560]{1,0:T(8,128)(2,1)} async-done(((bf16[256,2560]{1,0:T(8,128)(2,1)}), bf16[1024,2560]{1,0:T(8,128)(2,1)}) %all-gather.29.cloned.1.call-update) | async-done | bytes 5242896 | tf_op jit(solution)/shard_map/all_gather | solution.py:307
  1379.7 329.2 %all-reduce.8.cloned.1.call-done = (bf16[256,2048]{1,0:T(8,128)(2,1)}, bf16[256,11264]{1,0:T(8,128)(2,1)}, bf16[704,2048]{1,0:T(8,128)(2,1)}) async-done(((bf16[256,2048]{1,0:T(8,128)(2,1)}, bf16[256,11264]{1,0:T(8,128)(2,1)}, bf16[704,2048]{1,0:T(8,128)(2,1)}), (bf16[256,2048]{1,0:T(8,128)(2,1)}, bf16[256,11264]{1,0:T(8,128)(2,1)}, bf16[704,2048]{1,0:T(8,128)(2,1)})) %all-reduce.8.cloned.1.call-update) | async-done | bytes 9699344 | tf_op jit(solution)/shard_map/psum | solution.py:311
  1711.6 8.8 fusion.111
  (258 shorter events, 130.1 us)
Async XLA Ops:
  7.2 60.0 %copy-start = (s32[4,8]{1,0:T(4,128)S(1)}, s32[4,8]{1,0:T(4,128)}, u32[]{:S(2)}) copy-start(s32[4,8]{1,0:T(4,128)} %param.18) | copy-start | bytes 388
  7.2 54.4 %copy-start.2 = (bf16[128,2048]{1,0:T(8,128)(2,1)S(1)}, bf16[128,2048]{1,0:T(8,128)(2,1)}, u32[]{:S(2)}) copy-start(bf16[128,2048]{1,0:T(8,128)(2,1)} %param.16) | copy-start | bytes 1572868
  7.2 28.9 %all-gather.15.cloned.1.call-start = ((), (), s32[]{:S(2)}) async-start(), calls=%async_computation.6 | async-start | bytes 1179648 | tf_op jit(solution)/shard_map/all_gather | solution.py:143
  7.9 53.6 %all-gather.17.cloned.1.call-start = ((), (), s32[]{:S(2)}) async-start(), calls=%async_computation.7 | async-start | bytes 1179648 | tf_op jit(solution)/shard_map/all_gather | solution.py:144
  8.7 78.9 %all-gather.19.cloned.1.call-start = ((), (), s32[]{:S(2)}) async-start(), calls=%async_computation.8 | async-start | bytes 1179648 | tf_op jit(solution)/shard_map/all_gather | solution.py:164
  19.8 124.0 %copy-start.29 = (f32[8,1,256]{2,1,0:T(1,128)}, f32[8,1,256]{2,1,0:T(1,128)S(1)}, u32[]{:S(2)}) copy-start(f32[8,1,256]{2,1,0:T(1,128)S(1)} %convert_element_type.162) | copy-start | bytes 24580
  19.9 130.8 %copy-start.21 = (f32[128,64]{0,1:T(8,128)}, f32[128,64]{0,1:T(8,128)S(1)}, u32[]{:S(2)}) copy-start(f32[128,64]{0,1:T(8,128)S(1)} %get-tuple-element.259) | copy-start | bytes 98308
  20.0 130.8 %copy-start.23 = (f32[128,64]{0,1:T(8,128)}, f32[128,64]{0,1:T(8,128)S(1)}, u32[]{:S(2)}) copy-start(f32[128,64]{0,1:T(8,128)S(1)} %get-tuple-element.258) | copy-start | bytes 98308
  21.3 122.4 %copy-start.32 = (f32[128]{0:T(128)}, f32[128]{0:T(128)S(1)}, u32[]{:S(2)}) copy-start(f32[128]{0:T(128)S(1)} %add_rsqrt_fusion.1) | copy-start | bytes 1540
  63.8 79.9 %all-gather.13.cloned.1.call-start = ((), (), s32[]{:S(2)}) async-start(), calls=%async_computation.5 | async-start | bytes 9437184 | tf_op jit(solution)/shard_map/all_gather | solution.py:142
  64.4 135.5 %all-gather.21.cloned.1.call-start = ((), (), s32[]{:S(2)}) async-start(), calls=%async_computation.9 | async-start | bytes 9437184 | tf_op jit(solution)/shard_map/all_gather | solution.py:145
  65.0 253.1 %all-gather.23.cloned.1.call-start = ((), (), s32[]{:S(2)}) async-start(), calls=%async_computation.10 | async-start | bytes 25952256 | tf_op jit(solution)/shard_map/all_gather | solution.py:179
  65.6 370.9 %all-gather.25.cloned.1.call-start = ((), (), s32[]{:S(2)}) async-start(), calls=%async_computation.11 | async-start | bytes 25952256 | tf_op jit(solution)/shard_map/all_gather | solution.py:180
  66.4 488.5 %all-gather.27.cloned.1.call-start = ((), (), s32[]{:S(2)}) async-start(), calls=%async_computation.12 | async-start | bytes 25952256 | tf_op jit(solution)/shard_map/all_gather | solution.py:181
  67.1 623.8 %reduce-scatter.16.cloned.1.call-start = ((), (), s32[]{:S(2)}) async-start(), calls=%async_computation.17 | async-start | bytes 1179648
  168.4 36.2 %copy-start.5 = (bf16[128,2048]{0,1:T(8,128)(2,1)}, bf16[128,2048]{0,1:T(8,128)(2,1)S(1)}, u32[]{:S(2)}) copy-start(bf16[128,2048]{0,1:T(8,128)(2,1)S(1)} %fusion.88) | copy-start | bytes 1572868
  204.8 231.7 %copy-start.7 = (bf16[128,2048]{1,0:T(8,128)(2,1)}, bf16[128,2048]{1,0:T(8,128)(2,1)S(1)}, u32[]{:S(2)}) copy-start(bf16[128,2048]{1,0:T(8,128)(2,1)S(1)} %multiply_convert_fusion.4) | copy-start | bytes 1572868
  330.4 224.4 %copy-start.17 = (bf16[128,2048]{1,0:T(8,128)(2,1)S(1)}, bf16[128,2048]{1,0:T(8,128)(2,1)}, u32[]{:S(2)}) copy-start(bf16[128,2048]{1,0:T(8,128)(2,1)} %param.17) | copy-start | bytes 1572868
  569.8 12.3 copy-start.4
  654.7 125.9 %reduce-scatter.10.cloned.1.call-start = ((), (), s32[]{:S(2)}) async-start(), calls=%async_computation.13 | async-start | bytes 11796480 | tf_op jit(solution)/shard_map/reduce_scatter | solution.py:275
  656.2 35.9 %copy-start.30 = (f32[8,1,256]{2,1,0:T(1,128)S(1)}, f32[8,1,256]{2,1,0:T(1,128)}, u32[]{:S(2)}) copy-start(f32[8,1,256]{2,1,0:T(1,128)} %copy-done.29) | copy-start | bytes 24580
  656.3 35.9 %copy-start.33 = (f32[128]{0:T(128)S(1)}, f32[128]{0:T(128)}, u32[]{:S(2)}) copy-start(f32[128]{0:T(128)} %copy-done.32) | copy-start | bytes 1540
  656.6 42.3 %copy-start.11 = (bf16[128,2048]{0,1:T(8,128)(2,1)}, bf16[128,2048]{0,1:T(8,128)(2,1)S(1)}, u32[]{:S(2)}) copy-start(bf16[128,2048]{0,1:T(8,128)(2,1)S(1)} %fusion.87) | copy-start | bytes 1572868
  698.9 156.5 %reduce-scatter.12.cloned.1.call-start = ((), (), s32[]{:S(2)}) async-start(), calls=%async_computation.14 | async-start | bytes 9437184 | tf_op jit(solution)/shard_map/reduce_scatter | solution.py:283
  705.9 299.3 %reduce-scatter.14.cloned.1.call-start = ((), (), s32[]{:S(2)}) async-start(), calls=%async_computation.15 | async-start | bytes 25952256 | tf_op jit(solution)/shard_map/reduce_scatter | solution.py:299
  721.1 552.5 %reduce-scatter.18.cloned.1.call-start = ((), (), s32[]{:S(2)}) async-start(), calls=%async_computation.18 | async-start | bytes 51904512
  742.5 630.8 %all-gather.29.cloned.1.call-start = ((), (), s32[]{:S(2)}) async-start(), calls=%async_computation.16 | async-start | bytes 6553600 | tf_op jit(solution)/shard_map/all_gather | solution.py:307
  780.6 928.2 %all-reduce.8.cloned.1.call-start = ((), (), s32[]{:S(2)}) async-start(), calls=%async_computation.19 | async-start | bytes 19398656 | tf_op jit(solution)/shard_map/psum | solution.py:311
  1281.9 12.6 copy-start.19
  1282.0 13.1 copy-start.20
  1282.0 13.1 copy-start.31
  1711.6 8.8 copy-start.14
  (34 other events, 69.4 us)
Sparse Core Ops, SparseCore 0:
  9.9 26.1 all-gather.14
  38.0 23.4 all-gather.16
  64.0 23.4 all-gather.18
  89.3 54.3 all-gather.12
  145.5 54.3 all-gather.20
  201.6 116.4 all-gather.22
  320.0 116.4 all-gather.24
  438.4 116.4 all-gather.26
  654.8 36.0 reduce-scatter.15
  699.0 81.5 reduce-scatter.9
  784.1 71.2 reduce-scatter.11
  859.3 145.8 reduce-scatter.13
  1009.2 264.2 reduce-scatter.17
  1275.0 98.2 all-gather.28
  1376.0 332.8 all-reduce.7
